TPU v7x, 32 devices: a whole 2x2x4 slice. The times are simulated.
32 devices in a mesh: pipe: 4 (over x, core), rep: 8 (over z, y).
Axes of the slice: x: 2, y: 2, z: 4, core: 2. Of those that a mesh axis runs over, the one named last changes fastest.
Arguments:
- activations: bfloat16 [4, 8, 1, 8, 32, 384], P('pipe', 'rep'), may hold values from -8 to 8, as said below
- preactivation: bfloat16 [4, 8, 1, 8, 32, 384], P('pipe', 'rep'), may hold values from -6 to 6
- upstream: bfloat16 [4, 8, 1, 8, 32, 384], P('pipe', 'rep'), may hold values from -12 to 12, as said below
- weights: bfloat16 [4, 3456, 384], P('pipe'), may hold values from -0.109375 to 0.109375
- master: float32 [4, 8, 165888], P('pipe', 'rep'), may hold values from -0.3125 to 0.3125
- momentum: float32 [4, 8, 165888], P('pipe', 'rep'), may hold values from -6 to 6
Outputs:
- passed_grad: bfloat16 [4, 8, 1, 8, 32, 384], P('pipe', 'rep')
- new_momentum: float32 [4, 8, 165888], P('pipe', 'rep')
- new_weights: float32 [4, 8, 165888], P('pipe', 'rep')
Inputs may be any that keep to these rules, and one draw needn't show every extreme that they name: `activations`: Normal-like values; replicas of one section share part of their values. `upstream`: Normal-like values with a scale that differs from replica to replica; replicas of one section share part of their values.
All inputs are finite; a program needn't handle non-finite values.
Results may differ from a plain program's by a relative error of at most 0.0057.
Values may be sent and summed in bfloat16 or wider, within the bound.
A program may use at most 64 MiB of HBM per device.

v0:
```python
import jax
import jax.numpy as jnp
from jax import lax
from jax.sharding import PartitionSpec as P

EPS = 1e-06


def swapped(shard, axis, stride):
    return lax.ppermute(shard, axis, [(i, i ^ 1 << stride) for i in range(lax.axis_size(axis))])


def from_behind(shard, axis, by):
    count = lax.axis_size(axis)
    pairs = [(i, i + by) for i in range(count) if 0 <= i + by < count]
    return lax.ppermute(shard, axis, pairs)


def shifted_patches(tile_data, flipped):
    frames, tile_rows, tile_cols, channels = tile_data.shape
    padded = jnp.pad(tile_data, ((0, 0), (1, 1), (1, 1), (0, 0)))
    if flipped:
        offsets = [(2 - row_off, 2 - col_off) for row_off in range(3) for col_off in range(3)]
    else:
        offsets = [(row_off, col_off) for row_off in range(3) for col_off in range(3)]
    pieces = [
        padded[:, first : first + tile_rows, second : second + tile_cols, :]
        for first, second in offsets
    ]
    return jnp.concatenate(pieces, axis=-1).reshape(frames * tile_rows * tile_cols, 9 * channels)


def local_backward(tile_data, preact_tile, upstream_tile, kernel):
    frames, tile_rows, tile_cols, channels = tile_data.shape
    pre_float = preact_tile.astype(jnp.float32)
    sigmoid_val = jax.nn.sigmoid(pre_float)
    local_grad = (
        upstream_tile.astype(jnp.float32) * sigmoid_val * (1.0 + pre_float * (1.0 - sigmoid_val))
    ).astype(jnp.bfloat16)
    flat_grad = local_grad.reshape(-1, channels)
    patches = shifted_patches(tile_data, False)
    weight_grad = lax.dot_general(
        patches, flat_grad, (((0,), (0,)), ((), ())), preferred_element_type=jnp.float32
    ).astype(jnp.bfloat16)
    grad_patches = shifted_patches(local_grad, True).reshape(-1, 9, channels)
    kernel_taps = kernel.reshape(9, channels, channels)
    summed = lax.dot_general(
        grad_patches, kernel_taps, (((1, 2), (0, 2)), ((), ())), preferred_element_type=jnp.float32
    )
    return (
        weight_grad,
        summed.astype(jnp.bfloat16).reshape(frames, tile_rows, tile_cols, channels),
    )


def group_sum(partials, sum_bits):
    for bit_number in range(sum_bits):
        partials = partials + swapped(partials, "rep", bit_number)
    return partials


def body(activations, preactivation, upstream, weights, master, momentum):
    weight_grad, input_grad = local_backward(
        activations[0, 0], preactivation[0, 0], upstream[0, 0], weights[0]
    )
    passed = from_behind(input_grad, "pipe", -1)
    replicas = lax.axis_size("rep")
    level_count = replicas.bit_length() - 1
    rep_index = lax.axis_index("rep")
    held_rows = weight_grad.reshape(replicas, -1)
    for level_num in range(level_count):
        is_lower = jnp.right_shift(rep_index, level_num) & 1 == 0
        paired = held_rows.reshape(-1, 2, held_rows.shape[1])
        keep_rows = jnp.where(is_lower, paired[:, 0], paired[:, 1])
        give_rows = jnp.where(is_lower, paired[:, 1], paired[:, 0])
        other_rows = swapped(give_rows, "rep", level_num)
        keep_float = keep_rows.astype(jnp.float32)
        other_float = other_rows.astype(jnp.float32)
        keep_sq = jnp.sum(keep_float * keep_float)
        other_sq = jnp.sum(other_float * other_float)
        partials = jnp.stack(
            [
                jnp.where(is_lower, keep_sq, other_sq),
                jnp.where(is_lower, other_sq, keep_sq),
                jnp.sum(keep_float * other_float),
            ]
        )
        sum_bits = level_num + 1
        partials = group_sum(partials, sum_bits)
        lower_coef = 1.0 - partials[2] / (2.0 * partials[0] + EPS)
        upper_coef = 1.0 - partials[2] / (2.0 * partials[1] + EPS)
        keep_coef = jnp.where(is_lower, lower_coef, upper_coef)
        other_coef = jnp.where(is_lower, upper_coef, lower_coef)
        merged = keep_coef * keep_rows.astype(jnp.float32) + other_coef * other_rows.astype(
            jnp.float32
        )
        held_rows = merged.astype(jnp.bfloat16)
    combined = held_rows.astype(jnp.float32).reshape(momentum.shape)
    new_momentum = 0.9 * momentum + 0.0625 * combined
    new_weights = master - 0.02 * new_momentum
    return (passed[None, None], new_momentum, new_weights)


def solution(mesh):
    return jax.shard_map(
        body,
        mesh=mesh,
        in_specs=(
            P("pipe", "rep", None, None, None, None),
            P("pipe", "rep", None, None, None, None),
            P("pipe", "rep", None, None, None, None),
            P("pipe", None, None),
            P("pipe", "rep", None),
            P("pipe", "rep", None),
        ),
        out_specs=(
            P("pipe", "rep", None, None, None, None),
            P("pipe", "rep", None),
            P("pipe", "rep", None),
        ),
        check_vma=False,
    )
```

profile of v0, /device:TPU:0, one launch (start us, length us, event | category | flops | bytes accessed | tf_op | source)
XLA Modules:
  0.0 185.6 jit_solution(10420332771598263840)
XLA Ops:
  6.0 2.8 %fusion = bf16[3456,384]{1,0:T(8,128)(2,1)} fusion(bf16[1,8,32,3456]{3,2,1,0:T(8,128)(2,1)S(1)} %fusion.56, bf16[1,1,1,8,32,384]{5,4,3,2,1,0:T(8,128)(2,1)S(1)} %copy-done.5, bf16[1,1,1,8,32,384]{5,4,3,2,1,0:T(8,128)(2,1)S(1)} %copy-done.6), kind=kOutput, calls=%fused_computation.1 | convolution fusion | flops 681885696 | bytes 4816896 | tf_op jit(solution)/shard_map/dot_general | solution.py:42
  8.7 4.3 %reshape_reshape.7 = bf16[4,2,165888]{2,1,0:T(2,128)(2,1)} reshape(bf16[3456,384]{1,0:T(8,128)(2,1)} %fusion) | data formatting | bytes 5308416 | tf_op jit(solution)/shard_map/reshape;reshape | solution.py:73
  13.0 8.2 %fusion.62 = (bf16[4,1,165888]{2,1,0:T(2,128)(2,1)}, bf16[4,1,165888]{2,1,0:T(2,128)(2,1)}) fusion(bf16[4,2,165888]{2,1,0:T(2,128)(2,1)} %reshape_reshape.7), kind=kLoop, calls=%fused_computation.103 | loop fusion | bytes 5308416 | tf_op jit(solution)/shard_map/slice | solution.py:74
  21.2 6.0 %select_bitcast_fusion = bf16[4,165888]{1,0:T(4,128)(2,1)} fusion(pred[]{:T(512)S(6)} %eq.11, bf16[4,1,165888]{2,1,0:T(2,128)(2,1)} %get-tuple-element.18, bf16[4,1,165888]{2,1,0:T(2,128)(2,1)} %get-tuple-element.17), kind=kLoop, calls=%fused_computation.25 | loop fusion | flops 663552 | bytes 3981313 | tf_op jit(solution)/shard_map/jit(_where)/select_n | solution.py:75
  27.3 3.0 %collective-permute-start.1 = (bf16[4,165888]{1,0:T(4,128)(2,1)}, bf16[4,165888]{1,0:T(4,128)(2,1)}, u32[]{:S(2)}, u32[]{:S(2)}) collective-permute-start(bf16[4,165888]{1,0:T(4,128)(2,1)} %select_bitcast_fusion), channel_id=1, source_target_pairs={{0,1},{1,0},{2,3},{3,2},{4,5},{5,4},{6,7},{7,6},{8,9},{9,8},{10,11... | collective-permute-start | bytes 3981320 | tf_op jit(solution)/shard_map/ppermute | solution.py:10
  32.7 27.0 %collective-permute-done.1 = bf16[4,165888]{1,0:T(4,128)(2,1)} collective-permute-done((bf16[4,165888]{1,0:T(4,128)(2,1)}, bf16[4,165888]{1,0:T(4,128)(2,1)}, u32[]{:S(2)}, u32[]{:S(2)}) %collective-permute-start.1) | collective-permute-done | bytes 1327136 | tf_op jit(solution)/shard_map/ppermute | solution.py:10
  59.7 6.8 %fusion.4 = (f32[]{:T(128)}, f32[]{:T(128)}, f32[]{:T(128)}, bf16[4,1,165888]{2,0,1:T(4,128)(2,1)}) fusion(bf16[4,165888]{1,0:T(4,128)(2,1)} %collective-permute-done.1, bf16[4,1,165888]{2,1,0:T(2,128)(2,1)} %get-tuple-element.18, bf16[4,1,165888]{2,1,0:T(2,128)(2,1)} %get-tuple-element.17, pred[]{:T(512)S(6)} %eq.11), kind=kLoop, calls=%fused_computation.10 | loop fusion | flops 5971965 | bytes 5308429 | tf_op jit(solution)/shard_map/reduce_sum | solution.py:79
  77.4 3.2 %fusion.3 = bf16[4,165888]{1,0:T(4,128)(2,1)} fusion(bf16[4,165888]{1,0:T(4,128)(2,1)} %collective-permute-done.1, bf16[4,1,165888]{2,0,1:T(4,128)(2,1)} %get-tuple-element.16, f32[]{:T(128)S(6)} %select_n.118, f32[]{:T(128)S(6)} %select_n.117), kind=kLoop, calls=%fused_computation.9 | loop fusion | flops 3981312 | bytes 3981320 | tf_op jit(solution)/shard_map/convert_element_type | solution.py:97
  80.6 3.1 %reshape.237 = bf16[2,2,165888]{2,1,0:T(2,128)(2,1)} reshape(bf16[4,165888]{1,0:T(4,128)(2,1)} %fusion.3) | data formatting | bytes 2654208 | tf_op jit(solution)/shard_map/reshape | solution.py:73
  83.6 3.9 %fusion.63 = (bf16[2,1,165888]{2,1,0:T(2,128)(2,1)S(1)}, bf16[2,1,165888]{2,1,0:T(2,128)(2,1)S(1)}) fusion(bf16[2,2,165888]{2,1,0:T(2,128)(2,1)} %reshape.237), kind=kLoop, calls=%fused_computation.104 | loop fusion | bytes 2654208 | tf_op jit(solution)/shard_map/slice | solution.py:74
  87.5 2.6 %fusion.24 = bf16[2,165888]{1,0:T(2,128)(2,1)} fusion(pred[]{:T(512)S(6)} %eq.10, bf16[2,1,165888]{2,1,0:T(2,128)(2,1)S(1)} %get-tuple-element.20, bf16[2,1,165888]{2,1,0:T(2,128)(2,1)S(1)} %get-tuple-element.19), kind=kLoop, calls=%fused_computation.37 | loop fusion | flops 331776 | bytes 1990657 | tf_op jit(solution)/shard_map/jit(_where)/select_n | solution.py:75
  96.4 4.8 %reshape_reshape.6 = bf16[256,9,384]{2,1,0:T(8,128)(2,1)} reshape(bf16[1,8,32,3456]{3,2,1,0:T(8,128)(2,1)} %fusion.48) | data formatting | bytes 3538944 | tf_op jit(solution)/shard_map/reshape;reshape | solution.py:45
  101.3 4.0 %collective-permute-done.3 = bf16[2,165888]{1,0:T(2,128)(2,1)S(1)} collective-permute-done((bf16[2,165888]{1,0:T(2,128)(2,1)}, bf16[2,165888]{1,0:T(2,128)(2,1)S(1)}, u32[]{:S(2)}, u32[]{:S(2)}) %collective-permute-start.3) | collective-permute-done | bytes 663584 | tf_op jit(solution)/shard_map/ppermute | solution.py:10
  105.3 6.4 %fusion.12 = (f32[]{:T(128)}, f32[]{:T(128)}, f32[]{:T(128)}, bf16[2,165888]{1,0:T(2,128)(2,1)}) fusion(bf16[2,165888]{1,0:T(2,128)(2,1)S(1)} %collective-permute-done.3, bf16[2,1,165888]{2,1,0:T(2,128)(2,1)} %copy-done.3, bf16[2,1,165888]{2,1,0:T(2,128)(2,1)} %copy-done.2, pred[]{:T(512)S(6)} %eq.10), kind=kLoop, calls=%fused_computation.23 | loop fusion | flops 2985981 | bytes 2654221 | tf_op jit(solution)/shard_map/reduce_sum | solution.py:79
  116.5 2.1 %collective-permute-done.4 = f32[3]{0:T(128)S(1)} collective-permute-done((f32[3]{0:T(128)S(1)}, f32[3]{0:T(128)S(1)}, u32[]{:S(2)}, u32[]{:S(2)}) %collective-permute-start.4) | collective-permute-done | bytes 44 | tf_op jit(solution)/shard_map/ppermute | solution.py:10
  120.8 2.1 %collective-permute-done.5 = f32[3]{0:T(128)S(1)} collective-permute-done((f32[3]{0:T(128)S(1)}, f32[3]{0:T(128)S(1)}, u32[]{:S(2)}, u32[]{:S(2)}) %collective-permute-start.5) | collective-permute-done | bytes 44 | tf_op jit(solution)/shard_map/ppermute | solution.py:10
  126.6 2.4 %fusion.25 = bf16[1,2,165888]{2,1,0:T(2,128)(2,1)S(1)} fusion(bf16[2,165888]{1,0:T(2,128)(2,1)S(1)} %collective-permute-done.3, f32[]{:T(128)S(6)} %select_n.125, bf16[2,165888]{1,0:T(2,128)(2,1)} %get-tuple-element.15, f32[]{:T(128)S(6)} %select_n.124), kind=kLoop, calls=%fused_computation.43 | loop fusion | flops 1990656 | bytes 1990664 | tf_op jit(solution)/shard_map/reshape | solution.py:73
  130.2 2.6 %collective-permute-start.6 = (bf16[1,165888]{1,0:T(2,128)(2,1)S(1)}, bf16[1,165888]{1,0:T(2,128)(2,1)S(1)}, u32[]{:S(2)}, u32[]{:S(2)}) collective-permute-start(bf16[1,165888]{1,0:T(2,128)(2,1)S(1)} %fusion.22), channel_id=1, source_target_pairs={{0,4},{1,5},{2,6},{3,7},{4,0},{5,1},{6,2},{7,3},{8,12},{9,13},{10,... | collective-permute-start | bytes 995336 | tf_op jit(solution)/shard_map/ppermute | solution.py:10
  137.2 19.9 %collective-permute-done.6 = bf16[1,165888]{1,0:T(2,128)(2,1)S(1)} collective-permute-done((bf16[1,165888]{1,0:T(2,128)(2,1)S(1)}, bf16[1,165888]{1,0:T(2,128)(2,1)S(1)}, u32[]{:S(2)}, u32[]{:S(2)}) %collective-permute-start.6) | collective-permute-done | bytes 331808 | tf_op jit(solution)/shard_map/ppermute | solution.py:10
  157.1 3.8 %multiply_reduce_fusion.2 = (f32[]{:T(128)}, f32[]{:T(128)}, f32[]{:T(128)}, f32[1,165888]{1,0:T(1,128)}) fusion(bf16[1,165888]{1,0:T(2,128)(2,1)S(1)} %collective-permute-done.6, bf16[1,2,165888]{2,1,0:T(2,128)(2,1)S(1)} %fusion.25, pred[]{:T(512)S(6)} %eq.9), kind=kLoop, calls=%fused_computation.42 | loop fusion | flops 1492989 | bytes 1658893 | tf_op jit(solution)/shard_map/reduce_sum | solution.py:79
  165.5 2.4 %collective-permute-done.7 = f32[3]{0:T(128)S(1)} collective-permute-done((f32[3]{0:T(128)S(1)}, f32[3]{0:T(128)S(1)}, u32[]{:S(2)}, u32[]{:S(2)}) %collective-permute-start.7) | collective-permute-done | bytes 44 | tf_op jit(solution)/shard_map/ppermute | solution.py:10
  169.0 3.2 %collective-permute-done.8 = f32[3]{0:T(128)S(1)} collective-permute-done((f32[3]{0:T(128)S(1)}, f32[3]{0:T(128)S(1)}, u32[]{:S(2)}, u32[]{:S(2)}) %collective-permute-start.8) | collective-permute-done | bytes 44 | tf_op jit(solution)/shard_map/ppermute | solution.py:10
  174.6 2.8 %collective-permute-done.9 = f32[3]{0:T(128)S(1)} collective-permute-done((f32[3]{0:T(128)S(1)}, f32[3]{0:T(128)S(1)}, u32[]{:S(2)}, u32[]{:S(2)}) %collective-permute-start.9) | collective-permute-done | bytes 44 | tf_op jit(solution)/shard_map/ppermute | solution.py:10
  180.8 4.1 %multiply_subtract_fusion = (f32[1,1,165888]{2,1,0:T(1,128)}, f32[1,1,165888]{2,1,0:T(1,128)}) fusion(f32[1,1,165888]{2,1,0:T(1,128)} %param.10, bf16[1,165888]{1,0:T(2,128)(2,1)S(1)} %collective-permute-done.6, f32[]{:T(128)S(6)} %select_n.132, f32[1,165888]{1,0:T(1,128)} %get-tuple-element.14, f32[]{:T(128)S(6)} %select_n.131, f32[1,1,165888]{2,1,0:T(1,128)} %param.11), kind=kLoop, calls=%fused_computation.39 | loop fusion | flops 1824768 | bytes 3649544 | tf_op jit(solution)/shard_map/sub | solution.py:100
  (58 shorter events, 37.6 us)
Async XLA Ops:
  0.6 132.1 %copy-start = (bf16[1,3456,384]{2,1,0:T(8,128)(2,1)S(1)}, bf16[1,3456,384]{2,1,0:T(8,128)(2,1)}, u32[]{:S(2)}) copy-start(bf16[1,3456,384]{2,1,0:T(8,128)(2,1)} %param.9) | copy-start | bytes 7962628
  0.6 5.1 %copy-start.1 = (bf16[1,1,1,8,32,384]{5,4,3,2,1,0:T(8,128)(2,1)S(1)}, bf16[1,1,1,8,32,384]{5,4,3,2,1,0:T(8,128)(2,1)}, u32[]{:S(2)}) copy-start(bf16[1,1,1,8,32,384]{5,4,3,2,1,0:T(8,128)(2,1)} %param.6) | copy-start | bytes 589828
  0.7 5.3 %copy-start.5 = (bf16[1,1,1,8,32,384]{5,4,3,2,1,0:T(8,128)(2,1)S(1)}, bf16[1,1,1,8,32,384]{5,4,3,2,1,0:T(8,128)(2,1)}, u32[]{:S(2)}) copy-start(bf16[1,1,1,8,32,384]{5,4,3,2,1,0:T(8,128)(2,1)} %param.8) | copy-start | bytes 589828
  0.7 5.3 %copy-start.6 = (bf16[1,1,1,8,32,384]{5,4,3,2,1,0:T(8,128)(2,1)S(1)}, bf16[1,1,1,8,32,384]{5,4,3,2,1,0:T(8,128)(2,1)}, u32[]{:S(2)}) copy-start(bf16[1,1,1,8,32,384]{5,4,3,2,1,0:T(8,128)(2,1)} %param.7) | copy-start | bytes 589828
  27.3 32.4 %collective-permute-start.1 = (bf16[4,165888]{1,0:T(4,128)(2,1)}, bf16[4,165888]{1,0:T(4,128)(2,1)}, u32[]{:S(2)}, u32[]{:S(2)}) collective-permute-start(bf16[4,165888]{1,0:T(4,128)(2,1)} %select_bitcast_fusion), channel_id=1, source_target_pairs={{0,1},{1,0},{2,3},{3,2},{4,5},{5,4},{6,7},{7,6},{8,9},{9,8},{10,11... | collective-permute-start | bytes 3981320 | tf_op jit(solution)/shard_map/ppermute | solution.py:10
  69.9 3.6 %collective-permute-start.2 = (f32[3]{0:T(128)S(1)}, f32[3]{0:T(128)S(1)}, u32[]{:S(2)}, u32[]{:S(2)}) collective-permute-start(f32[3]{0:T(128)S(1)} %pad_maximum_fusion), channel_id=1, source_target_pairs={{0,1},{1,0},{2,3},{3,2},{4,5},{5,4},{6,7},{7,6},{8,9},{9,8},{10,11... | collective-permute-start | bytes 44 | tf_op jit(solution)/shard_map/ppermute | solution.py:10
  87.5 5.2 %copy-start.2 = (bf16[2,1,165888]{2,1,0:T(2,128)(2,1)}, bf16[2,1,165888]{2,1,0:T(2,128)(2,1)S(1)}, u32[]{:S(2)}) copy-start(bf16[2,1,165888]{2,1,0:T(2,128)(2,1)S(1)} %get-tuple-element.19) | copy-start | bytes 1990660
  87.5 5.2 %copy-start.3 = (bf16[2,1,165888]{2,1,0:T(2,128)(2,1)}, bf16[2,1,165888]{2,1,0:T(2,128)(2,1)S(1)}, u32[]{:S(2)}) copy-start(bf16[2,1,165888]{2,1,0:T(2,128)(2,1)S(1)} %get-tuple-element.20) | copy-start | bytes 1990660
  90.1 15.1 %collective-permute-start.3 = (bf16[2,165888]{1,0:T(2,128)(2,1)}, bf16[2,165888]{1,0:T(2,128)(2,1)S(1)}, u32[]{:S(2)}, u32[]{:S(2)}) collective-permute-start(bf16[2,165888]{1,0:T(2,128)(2,1)} %fusion.24), channel_id=1, source_target_pairs={{0,2},{1,3},{2,0},{3,1},{4,6},{5,7},{6,4},{7,5},{8,10},{9,11},{10,... | collective-permute-start | bytes 1990664 | tf_op jit(solution)/shard_map/ppermute | solution.py:10
  115.0 3.6 %collective-permute-start.4 = (f32[3]{0:T(128)S(1)}, f32[3]{0:T(128)S(1)}, u32[]{:S(2)}, u32[]{:S(2)}) collective-permute-start(f32[3]{0:T(128)S(1)} %pad_maximum_fusion.1), channel_id=1, source_target_pairs={{0,1},{1,0},{2,3},{3,2},{4,5},{5,4},{6,7},{7,6},{8,9},{9,8},{10,11... | collective-permute-start | bytes 44 | tf_op jit(solution)/shard_map/ppermute | solution.py:10
  119.3 3.6 %collective-permute-start.5 = (f32[3]{0:T(128)S(1)}, f32[3]{0:T(128)S(1)}, u32[]{:S(2)}, u32[]{:S(2)}) collective-permute-start(f32[3]{0:T(128)S(1)} %fusion.69), channel_id=1, source_target_pairs={{0,2},{1,3},{2,0},{3,1},{4,6},{5,7},{6,4},{7,5},{8,10},{9,11},{10,... | collective-permute-start | bytes 44 | tf_op jit(solution)/shard_map/ppermute | solution.py:10
  126.6 6.2 %copy-start.4 = (bf16[256,9,384]{2,1,0:T(8,128)(2,1)S(1)}, bf16[256,9,384]{2,1,0:T(8,128)(2,1)}, u32[]{:S(2)}) copy-start(bf16[256,9,384]{2,1,0:T(8,128)(2,1)} %reshape_reshape.6) | copy-start | bytes 5308420
  130.2 26.9 %collective-permute-start.6 = (bf16[1,165888]{1,0:T(2,128)(2,1)S(1)}, bf16[1,165888]{1,0:T(2,128)(2,1)S(1)}, u32[]{:S(2)}, u32[]{:S(2)}) collective-permute-start(bf16[1,165888]{1,0:T(2,128)(2,1)S(1)} %fusion.22), channel_id=1, source_target_pairs={{0,4},{1,5},{2,6},{3,7},{4,0},{5,1},{6,2},{7,3},{8,12},{9,13},{10,... | collective-permute-start | bytes 995336 | tf_op jit(solution)/shard_map/ppermute | solution.py:10
  133.9 3.3 %collective-permute-start = (bf16[1,8,32,384]{3,2,1,0:T(8,128)(2,1)S(1)}, bf16[1,8,32,384]{3,2,1,0:T(8,128)(2,1)S(1)}, u32[]{:S(2)}, u32[]{:S(2)}) collective-permute-start(bf16[1,8,32,384]{3,2,1,0:T(8,128)(2,1)S(1)} %bitcast.99), channel_id=1, source_target_pairs={{8,0},{16,8},{24,16},{9,1},{17,9},{25,17},{10,2},{18,10},{26,18},{... | collective-permute-start | bytes 589832 | tf_op jit(solution)/shard_map/ppermute | solution.py:16
  164.3 3.6 %collective-permute-start.7 = (f32[3]{0:T(128)S(1)}, f32[3]{0:T(128)S(1)}, u32[]{:S(2)}, u32[]{:S(2)}) collective-permute-start(f32[3]{0:T(128)S(1)} %pad_maximum_fusion.2), channel_id=1, source_target_pairs={{0,1},{1,0},{2,3},{3,2},{4,5},{5,4},{6,7},{7,6},{8,9},{9,8},{10,11... | collective-permute-start | bytes 44 | tf_op jit(solution)/shard_map/ppermute | solution.py:10
  168.6 3.6 %collective-permute-start.8 = (f32[3]{0:T(128)S(1)}, f32[3]{0:T(128)S(1)}, u32[]{:S(2)}, u32[]{:S(2)}) collective-permute-start(f32[3]{0:T(128)S(1)} %fusion.68), channel_id=1, source_target_pairs={{0,2},{1,3},{2,0},{3,1},{4,6},{5,7},{6,4},{7,5},{8,10},{9,11},{10,... | collective-permute-start | bytes 44 | tf_op jit(solution)/shard_map/ppermute | solution.py:10
  172.9 4.5 %collective-permute-start.9 = (f32[3]{0:T(128)S(1)}, f32[3]{0:T(128)S(1)}, u32[]{:S(2)}, u32[]{:S(2)}) collective-permute-start(f32[3]{0:T(128)S(1)} %fusion.71), channel_id=1, source_target_pairs={{0,4},{1,5},{2,6},{3,7},{4,0},{5,1},{6,2},{7,3},{8,12},{9,13},{10,... | collective-permute-start | bytes 44 | tf_op jit(solution)/shard_map/ppermute | solution.py:10
where the time goes:
time: 187 us; the launch traced here: 186 us
  waiting for transfers between devices  67.4 us (36%)
  other arithmetic  42.4 us (23%)
  local copies, waits for them, and re-layouts  38.8 us (21%)
  starting transfers between devices  16.6 us (9%)
  between operations  16.5 us (9%)
  matrix products  3.86 us (2%)
    ppermute x9, waiting for transfers between devices, swapped(): lax.ppermute(shard, axis, [(i, i ^ 1 << stride) for i in range(lax.axis_s...  65.3 us
    reduce_sum x3, other arithmetic, body(): keep_sq = jnp.sum(keep_float * keep_float)  17 us
    ppermute x9, starting transfers between devices, swapped(): lax.ppermute(shard, axis, [(i, i ^ 1 << stride) for i in range(lax.axis_s...  15.3 us
    slice x2, local copies, waits for them, and re-layouts, body(): keep_rows = jnp.where(is_lower, paired[:, 0], paired[:, 1])  12.1 us
    unnamed x31, local copies, waits for them, and re-layouts  11.8 us
    select_n x3, other arithmetic, body(): give_rows = jnp.where(is_lower, paired[:, 1], paired[:, 0])  9.8 us
    another operation x1, local copies, waits for them, and re-layouts, local_backward(): grad_patches = shifted_patches(local_grad, True).reshape(-1, 9, channels)  4.84 us
    another operation x1, local copies, waits for them, and re-layouts, body(): paired = held_rows.reshape(-1, 2, held_rows.shape[1])  4.3 us
  transfers between devices with their start and end apart: 10, of which 10 were waited for; matrix products, arithmetic and copies ran while one was open for 7% of the time, Pallas kernels for 0%

commit v1 on v0

--- a/solution.py
+++ b/solution.py
@@ -1,6 +1,10 @@
+import functools
+
 import jax
 import jax.numpy as jnp
 from jax import lax
+from jax.experimental import pallas as pl
+from jax.experimental.pallas import tpu as pltpu
 from jax.sharding import PartitionSpec as P
 
 EPS = 1e-06
@@ -100,10 +104,322 @@
     new_weights = master - 0.02 * new_momentum
     return (passed[None, None], new_momentum, new_weights)
 
+MESH = pl.DeviceIdType.MESH
+F32 = jnp.float32
+BF16 = jnp.bfloat16
+
+
+def chunk_rows(channels):
+    return next(rows for rows in (64, 48, 32, 16) if channels % rows == 0)
+
+
+def fold(product):
+    return jnp.sum(product.reshape(-1, 8, product.shape[-1]), axis=0)
+
+
+def pair_dots(lower, upper, rows_total, rows):
+    channels = lower.shape[-1]
+
+    def step(i, sums):
+        here = pl.ds(pl.multiple_of(i * rows, rows), rows)
+        a, b = lower[here, :].astype(F32), upper[here, :].astype(F32)
+        return sums[0] + fold(a * a), sums[1] + fold(b * b), sums[2] + fold(a * b)
+
+    zero = jnp.zeros((8, channels), F32)
+    aa, bb, ab = lax.fori_loop(0, rows_total // rows, step, (zero, zero, zero))
+    aa, bb, ab = jnp.sum(aa), jnp.sum(bb), jnp.sum(ab)
+    return 1.0 - ab / (2.0 * aa + EPS), 1.0 - ab / (2.0 * bb + EPS)
+
+
+def pair_merge(lower, upper, target, coefs, rows_total, rows):
+    def step(i, carry):
+        here = pl.ds(pl.multiple_of(i * rows, rows), rows)
+        a, b = lower[here, :].astype(F32), upper[here, :].astype(F32)
+        target[here, :] = (coefs[0] * a + coefs[1] * b).astype(BF16)
+        return carry
+
+    lax.fori_loop(0, rows_total // rows, step, 0)
+
+
+def kernel(
+    sections, replicas, cols,
+    act_ref, pre_ref, up_ref, weights_hbm, master_hbm, momentum_hbm,
+    passed_ref, new_mom_ref, new_w_ref,
+    factors, shifted, xt, kernel_v, igrad, pair_w, merged, master_v, momentum_v,
+    send_sem, recv_sem, pass_sem, load_sem,
+):
+    pixels, channels = act_ref.shape
+    rows_total = kernel_v.shape[0]
+    rows = chunk_rows(channels)
+    pipe, rep = lax.axis_index("pipe"), lax.axis_index("rep")
+    chain = replicas // 2
+    z, y = rep // 2, rep % 2
+    other = z * 2 + 1 - y
+
+    barrier = pltpu.get_barrier_semaphore()
+
+    def greet(cond, device):
+        @pl.when(cond)
+        def _():
+            pl.semaphore_signal(barrier, inc=1, device_id=device, device_id_type=MESH)
+
+    pl.semaphore_signal(barrier, inc=1, device_id=(pipe, other), device_id_type=MESH)
+    greet(z > 0, (pipe, rep - 2))
+    greet(z < chain - 1, (pipe, rep + 2))
+    greet(pipe < sections - 1, (pipe + 1, rep))
+
+    loads = [
+        pltpu.make_async_copy(src, dst, load_sem.at[i])
+        for i, (src, dst) in enumerate(
+            ((weights_hbm, kernel_v), (master_hbm, master_v), (momentum_hbm, momentum_v))
+        )
+    ]
+    for load in loads:
+        load.start()
+
+    z_f = pre_ref[...].astype(F32)
+    sig = jax.nn.sigmoid(z_f)
+    factors[rep, 1] = (up_ref[...].astype(F32) * sig * (1.0 + z_f * (1.0 - sig))).astype(BF16)
+    factors[rep, 0] = act_ref[...]
+
+    edge = jnp.zeros((cols, channels), BF16)
+    for j in range(3):
+        shifted[j, pl.ds(0, cols), :] = edge
+        shifted[j, pl.ds(cols + pixels, cols), :] = edge
+
+    def spread(block):
+        grad = factors[block, 1].astype(F32)
+        column = lax.broadcasted_iota(jnp.int32, (pixels, channels), 0) % cols
+        here = pl.ds(cols, pixels)
+        shifted[0, here, :] = jnp.where(
+            column < cols - 1, pltpu.roll(grad, pixels - 1, 0), 0.0
+        ).astype(BF16)
+        shifted[1, here, :] = factors[block, 1]
+        shifted[2, here, :] = jnp.where(column > 0, pltpu.roll(grad, 1, 0), 0.0).astype(BF16)
+
+    def tap(i, j):
+        return shifted[j, pl.ds((2 - i) * cols, pixels), :]
+
+    met = 1 + (z > 0).astype(jnp.int32) + (z < chain - 1).astype(jnp.int32)
+    pl.semaphore_wait(barrier, met + (pipe > 0).astype(jnp.int32))
+
+    def copy_of(block, half, way, target):
+        return pltpu.make_async_remote_copy(
+            src_ref=factors.at[block, half],
+            dst_ref=factors.at[block, half],
+            send_sem=send_sem.at[way, block, half],
+            recv_sem=recv_sem.at[block, half],
+            device_id=(pipe, target),
+            device_id_type=MESH,
+        )
+
+    def ways(source):
+        return (
+            (0, (source <= z) & (z < chain - 1), jnp.minimum(rep + 2, replicas - 1)),
+            (1, (source >= z) & (z > 0), jnp.maximum(rep - 2, 0)),
+        )
+
+    def order(k):
+        if k == 0:
+            return z
+        short = jnp.minimum(z, chain - 1 - z)
+        near = z - (k + 1) // 2 if k % 2 else z + k // 2
+        far = jnp.where(z <= chain - 1 - z, k, chain - 1 - k)
+        return jnp.where(k <= 2 * short, near, far)
+
+    sources = [order(k) for k in range(chain)]
+
+    def forward(k):
+        source = sources[k]
+        block = source * 2 + y
+        for half in range(2):
+            if k:
+                copy_of(block, half, 2, other).wait_recv()
+            for way, cond, target in ways(source):
+                @pl.when(cond)
+                def _():
+                    copy_of(block, half, way, target).start()
+            copy_of(block, half, 2, other).start()
+
+    def replica_grad(slot, block):
+        spread(block)
+        xt[...] = factors[block, 0].T
+        for i in range(3):
+            for j in range(3):
+                grad = jnp.dot(xt[...], tap(i, j), preferred_element_type=F32)
+                pair_w[slot, pl.ds((i * 3 + j) * channels, channels), :] = grad.astype(BF16)
+
+    def process(k):
+        source = sources[k]
+
+        def one(slot, carry):
+            block = source * 2 + jnp.where(slot == 0, y, 1 - y)
+
+            @pl.when(slot == 1)
+            def _():
+                for half in range(2):
+                    copy_of(block, half, 2, other).wait_recv()
+
+            replica_grad(jnp.where(slot == 0, y, 1 - y), block)
+            return carry
+
+        lax.fori_loop(0, 2, one, 0)
+        coefs = pair_dots(pair_w.at[0], pair_w.at[1], rows_total, rows)
+        pair_merge(pair_w.at[0], pair_w.at[1], merged.at[source], coefs, rows_total, rows)
+
+    forward(0)
+
+    spread(rep)
+    loads[0].wait()
+    total = jnp.zeros((pixels, channels), F32)
+    for i in range(3):
+        for j in range(3):
+            total = total + lax.dot_general(
+                tap(i, j),
+                kernel_v[pl.ds((i * 3 + j) * channels, channels), :],
+                (((1,), (1,)), ((), ())),
+                preferred_element_type=F32,
+            )
+    igrad[...] = total.astype(BF16)
+
+    @pl.when(pipe == sections - 1)
+    def _():
+        passed_ref[...] = jnp.zeros_like(passed_ref)
+
+    passing = pltpu.make_async_remote_copy(
+        src_ref=igrad,
+        dst_ref=passed_ref,
+        send_sem=pass_sem.at[0],
+        recv_sem=pass_sem.at[1],
+        device_id=(jnp.maximum(pipe - 1, 0), rep),
+        device_id_type=MESH,
+    )
+
+    for k in range(1, chain):
+        forward(k)
+        if k == 1:
+            @pl.when(pipe > 0)
+            def _():
+                passing.start()
+        process(k - 1)
+    if chain == 1:
+        @pl.when(pipe > 0)
+        def _():
+            passing.start()
+    process(chain - 1)
+
+    stride = 1
+    while stride * 2 < chain:
+        for low in range(0, chain, stride * 2):
+            pair = merged.at[low], merged.at[low + stride]
+            coefs = pair_dots(*pair, rows_total, rows)
+            pair_merge(*pair, merged.at[low], coefs, rows_total, rows)
+        stride *= 2
+    for load in loads[1:]:
+        load.wait()
+    own_rows = rows_total // replicas
+    own = pl.ds(pl.multiple_of(rep * own_rows, own_rows), own_rows)
+    if stride < chain:
+        coefs = pair_dots(merged.at[0], merged.at[stride], rows_total, rows)
+        final = coefs[0] * merged[0, own, :].astype(F32) + coefs[1] * merged[stride, own, :].astype(F32)
+        final = final.astype(BF16).astype(F32)
+    else:
+        final = merged[0, own, :].astype(F32)
+    lanes = momentum_v.shape[-1]
+    groups = channels // lanes
+    for g in range(groups):
+        at = pl.ds(g, own_rows, stride=groups)
+        momentum = 0.9 * momentum_v[at, :] + 0.0625 * final[:, g * lanes : (g + 1) * lanes]
+        new_mom_ref[at, :] = momentum
+        new_w_ref[at, :] = master_v[at, :] - 0.02 * momentum
+
+    for k in range(chain):
+        source = sources[k]
+        block = source * 2 + y
+        for half in range(2):
+            for way, cond, target in ways(source):
+                @pl.when(cond)
+                def _():
+                    copy_of(block, half, way, target).wait_send()
+            copy_of(block, half, 2, other).wait_send()
+
+    @pl.when(pipe > 0)
+    def _():
+        passing.wait_send()
+
+    @pl.when(pipe < sections - 1)
+    def _():
+        passing.wait_recv()
+
+
+def factor_body(sections, replicas, activations, preactivation, upstream, weights, master, momentum):
+    tile = activations.shape[3:]
+    cols, channels = tile[1], tile[2]
+    pixels = tile[0] * cols
+    taps_rows = weights.shape[1]
+    lanes = 128
+    flat = (momentum.shape[2] // lanes, lanes)
+    small, big = pl.BlockSpec(memory_space=pltpu.VMEM), pl.BlockSpec(memory_space=pl.ANY)
+    passed, new_momentum, new_weights = pl.pallas_call(
+        functools.partial(kernel, sections, replicas, cols),
+        out_shape=(
+            jax.ShapeDtypeStruct((pixels, channels), BF16),
+            jax.ShapeDtypeStruct(flat, F32),
+            jax.ShapeDtypeStruct(flat, F32),
+        ),
+        in_specs=[small, small, small, big, big, big],
+        out_specs=(small, small, small),
+        scratch_shapes=[
+            pltpu.VMEM((replicas, 2, pixels, channels), BF16),
+            pltpu.VMEM((3, pixels + 2 * cols, channels), BF16),
+            pltpu.VMEM((channels, pixels), BF16),
+            pltpu.VMEM((taps_rows, channels), BF16),
+            pltpu.VMEM((pixels, channels), BF16),
+            pltpu.VMEM((2, taps_rows, channels), BF16),
+            pltpu.VMEM((replicas // 2, taps_rows, channels), BF16),
+            pltpu.VMEM(flat, F32),
+            pltpu.VMEM(flat, F32),
+            pltpu.SemaphoreType.DMA((3, replicas, 2)),
+            pltpu.SemaphoreType.DMA((replicas, 2)),
+            pltpu.SemaphoreType.DMA((2,)),
+            pltpu.SemaphoreType.DMA((3,)),
+        ],
+        compiler_params=pltpu.CompilerParams(
+            collective_id=0, has_side_effects=True, vmem_limit_bytes=56 * 1024 * 1024
+        ),
+    )(
+        activations.reshape(pixels, channels),
+        preactivation.reshape(pixels, channels),
+        upstream.reshape(pixels, channels),
+        weights[0],
+        master.reshape(flat),
+        momentum.reshape(flat),
+    )
+    return (
+        passed.reshape(activations.shape),
+        new_momentum.reshape(momentum.shape),
+        new_weights.reshape(master.shape),
+    )
+
+
+def pick(sections, replicas, *arrays):
+    activations, weights, momentum = arrays[0], arrays[3], arrays[5]
+    factor = 2 * activations.size
+    fits = (
+        replicas >= 2
+        and activations.shape[2] == 1
+        and (replicas - 1) * factor <= 2 * weights.size
+        and activations.shape[4] % 16 == 0
+        and activations.shape[5] % 128 == 0
+        and (weights.shape[1] // replicas) % 16 == 0
+        and momentum.shape[2] % 1024 == 0
+    )
+    return factor_body(sections, replicas, *arrays) if fits else body(*arrays)
+
 
 def solution(mesh):
     return jax.shard_map(
-        body,
+        functools.partial(pick, mesh.shape["pipe"], mesh.shape["rep"]),
         mesh=mesh,
         in_specs=(
             P("pipe", "rep", None, None, None, None),

time: 187 us -> 62.5 us (0.33)
  waiting for transfers between devices: 67.4 us -> 0 us
  Pallas kernels: 0 us -> 56.4 us
  other arithmetic: 42.4 us -> 0 us
  local copies, waits for them, and re-layouts: 38.8 us -> 5.29 us
  starting transfers between devices: 16.6 us -> 0 us
  between operations: 16.5 us -> 0.64 us
  matrix products: 3.86 us -> 0 us
    ppermute x10 -> x0, waiting for transfers between devices: 67.4 us -> none  [the longest x9 65.3 us: swapped(): lax.ppermute(shard, axis, [(i, i ^ 1 << stride) for i in range(lax.axis_s...]
    pallas_call x0 -> x1, Pallas kernels: none -> 56.4 us  [factor_body(): pl.pallas_call(functools.partial(kernel, sections, replicas, cols), out_s...]
    reduce_sum x3 -> x0, other arithmetic: 17 us -> none  [body(): keep_sq = jnp.sum(keep_float * keep_float)]
    ppermute x10 -> x0, starting transfers between devices: 16.6 us -> none  [the longest x9 15.3 us: swapped(): lax.ppermute(shard, axis, [(i, i ^ 1 << stride) for i in range(lax.axis_s...]
    slice x5 -> x0, local copies, waits for them, and re-layouts: 14 us -> none  [the longest x2 12.1 us: body(): keep_rows = jnp.where(is_lower, paired[:, 0], paired[:, 1])]
    select_n x3 -> x0, other arithmetic: 9.8 us -> none  [body(): give_rows = jnp.where(is_lower, paired[:, 1], paired[:, 0])]
    another operation x2 -> x0, local copies, waits for them, and re-layouts: 9.14 us -> none  [the longest x1 4.84 us: local_backward(): grad_patches = shifted_patches(local_grad, True).reshape(-1, 9, channels)]
    unnamed x31 -> x3, local copies, waits for them, and re-layouts: 11.8 us -> 5.29 us
  transfers between devices with their start and end apart: 10 -> 0, of which waited for: 10 -> 0; matrix products, arithmetic and copies ran while one was open for 7% -> 0% of each run, Pallas kernels for 0% -> 0%
where the time goes in v1:
time: 62.5 us; the launch traced here: 62.3 us
  Pallas kernels  56.4 us (90%)
  local copies, waits for them, and re-layouts  5.29 us (8%)
  between operations  0.64 us (1%)
    pallas_call x1, Pallas kernels, factor_body(): pl.pallas_call(functools.partial(kernel, sections, replicas, cols), out_s...  56.4 us
    unnamed x3, local copies, waits for them, and re-layouts  5.29 us

profile of v1, /device:TPU:0, one launch (start us, length us, event | category | flops | bytes accessed | tf_op | source)
XLA Modules:
  0.0 62.3 jit_solution(2282508612051907668)
XLA Ops:
  0.6 56.4 %shard_map.85 = (bf16[256,384]{1,0:T(8,128)(2,1)}, f32[1296,128]{1,0:T(8,128)}, f32[1296,128]{1,0:T(8,128)}) custom-call(bf16[256,384]{1,0:T(8,128)(2,1)} %bitcast.14, bf16[256,384]{1,0:T(8,128)(2,1)} %bitcast.15, bf16[256,384]{1,0:T(8,128)(2,1)} %bitcast.16, bf16[3456,384]{1,0:T(8,128)(2,1)} %bitcast.9, f32[1296,128]{1,0:T(8,128)} %bitcast.10, ...), custom_call_target="tpu_custom_call" | custom-call | tf_op jit(solution)/shard_map/pallas_call | solution.py:363
  57.0 1.6 %copy.12 = bf16[1,1,1,8,32,384]{5,4,3,2,1,0:T(8,128)(2,1)} copy(bf16[1,1,1,8,32,384]{5,4,3,2,1,0:T(8,128)(2,1)} %bitcast.17) | data formatting | bytes 393216
  58.6 1.8 %copy.13 = f32[1,1,165888]{2,1,0:T(1,128)} copy(f32[1,1,165888]{2,1,0:T(1,128)} %bitcast.13) | data formatting | bytes 1327104
  60.5 1.8 %copy.14 = f32[1,1,165888]{2,1,0:T(1,128)} copy(f32[1,1,165888]{2,1,0:T(1,128)} %bitcast.12) | data formatting | bytes 1327104

commit v2 on v1

--- a/solution.py
+++ b/solution.py
@@ -117,35 +117,39 @@
     return jnp.sum(product.reshape(-1, 8, product.shape[-1]), axis=0)
 
 
-def pair_dots(lower, upper, rows_total, rows):
+def coefs_of(lower_sq, upper_sq, cross):
+    aa, bb, ab = jnp.sum(lower_sq), jnp.sum(upper_sq), jnp.sum(cross)
+    return 1.0 - ab / (2.0 * aa + EPS), 1.0 - ab / (2.0 * bb + EPS)
+
+
+def pair_merge(lower, upper, target, coefs, against, rows_total, rows):
     channels = lower.shape[-1]
 
     def step(i, sums):
         here = pl.ds(pl.multiple_of(i * rows, rows), rows)
         a, b = lower[here, :].astype(F32), upper[here, :].astype(F32)
-        return sums[0] + fold(a * a), sums[1] + fold(b * b), sums[2] + fold(a * b)
+        new = (coefs[0] * a + coefs[1] * b).astype(BF16)
+        target[here, :] = new
+        if against is None:
+            return sums
+        new, next_one = new.astype(F32), against[here, :].astype(F32)
+        return (
+            sums[0] + fold(new * new),
+            sums[1] + fold(next_one * next_one),
+            sums[2] + fold(new * next_one),
+        )
 
     zero = jnp.zeros((8, channels), F32)
-    aa, bb, ab = lax.fori_loop(0, rows_total // rows, step, (zero, zero, zero))
-    aa, bb, ab = jnp.sum(aa), jnp.sum(bb), jnp.sum(ab)
-    return 1.0 - ab / (2.0 * aa + EPS), 1.0 - ab / (2.0 * bb + EPS)
-
-
-def pair_merge(lower, upper, target, coefs, rows_total, rows):
-    def step(i, carry):
-        here = pl.ds(pl.multiple_of(i * rows, rows), rows)
-        a, b = lower[here, :].astype(F32), upper[here, :].astype(F32)
-        target[here, :] = (coefs[0] * a + coefs[1] * b).astype(BF16)
-        return carry
-
-    lax.fori_loop(0, rows_total // rows, step, 0)
+    init = () if against is None else (zero, zero, zero)
+    sums = lax.fori_loop(0, rows_total // rows, step, init)
+    return None if against is None else coefs_of(*sums)
 
 
 def kernel(
     sections, replicas, cols,
-    act_ref, pre_ref, up_ref, weights_hbm, master_hbm, momentum_hbm,
-    passed_ref, new_mom_ref, new_w_ref,
-    factors, shifted, xt, kernel_v, igrad, pair_w, merged, master_v, momentum_v,
+    act_ref, pre_ref, up_ref, weights_hbm,
+    passed_ref, combined_ref,
+    factors, shifted, xt, kernel_v, igrad, pair_w, merged,
     send_sem, recv_sem, pass_sem, load_sem,
 ):
     pixels, channels = act_ref.shape
@@ -168,18 +172,8 @@
     greet(z < chain - 1, (pipe, rep + 2))
     greet(pipe < sections - 1, (pipe + 1, rep))
 
-    loads = [
-        pltpu.make_async_copy(src, dst, load_sem.at[i])
-        for i, (src, dst) in enumerate(
-            ((weights_hbm, kernel_v), (master_hbm, master_v), (momentum_hbm, momentum_v))
-        )
-    ]
-    for load in loads:
-        load.start()
-
-    z_f = pre_ref[...].astype(F32)
-    sig = jax.nn.sigmoid(z_f)
-    factors[rep, 1] = (up_ref[...].astype(F32) * sig * (1.0 + z_f * (1.0 - sig))).astype(BF16)
+    load = pltpu.make_async_copy(weights_hbm, kernel_v, load_sem)
+    load.start()
     factors[rep, 0] = act_ref[...]
 
     edge = jnp.zeros((cols, channels), BF16)
@@ -222,17 +216,18 @@
     def order(k):
         if k == 0:
             return z
-        short = jnp.minimum(z, chain - 1 - z)
-        near = z - (k + 1) // 2 if k % 2 else z + k // 2
-        far = jnp.where(z <= chain - 1 - z, k, chain - 1 - k)
-        return jnp.where(k <= 2 * short, near, far)
+        size = 1 << (k.bit_length() - 1)
+        step, group = k - size, z // size
+        return jnp.where(
+            group % 2 == 0, (group + 1) * size + step, group * size - 1 - step
+        )
 
     sources = [order(k) for k in range(chain)]
 
-    def forward(k):
+    def forward(k, halves=(0, 1)):
         source = sources[k]
         block = source * 2 + y
-        for half in range(2):
+        for half in halves:
             if k:
                 copy_of(block, half, 2, other).wait_recv()
             for way, cond, target in ways(source):
@@ -244,33 +239,49 @@
     def replica_grad(slot, block):
         spread(block)
         xt[...] = factors[block, 0].T
+        own_sq = jnp.zeros((8, channels), F32)
+        cross = jnp.zeros((8, channels), F32)
         for i in range(3):
             for j in range(3):
-                grad = jnp.dot(xt[...], tap(i, j), preferred_element_type=F32)
-                pair_w[slot, pl.ds((i * 3 + j) * channels, channels), :] = grad.astype(BF16)
+                here = pl.ds((i * 3 + j) * channels, channels)
+                grad = jnp.dot(xt[...], tap(i, j), preferred_element_type=F32).astype(BF16)
+                pair_w[slot, here, :] = grad
+                grad = grad.astype(F32)
+                own_sq = own_sq + fold(grad * grad)
+                if slot:
+                    cross = cross + fold(grad * pair_w[0, here, :].astype(F32))
+        return own_sq, cross
+
+    stack = []
 
     def process(k):
         source = sources[k]
-
-        def one(slot, carry):
-            block = source * 2 + jnp.where(slot == 0, y, 1 - y)
-
-            @pl.when(slot == 1)
-            def _():
-                for half in range(2):
-                    copy_of(block, half, 2, other).wait_recv()
-
-            replica_grad(jnp.where(slot == 0, y, 1 - y), block)
-            return carry
-
-        lax.fori_loop(0, 2, one, 0)
-        coefs = pair_dots(pair_w.at[0], pair_w.at[1], rows_total, rows)
-        pair_merge(pair_w.at[0], pair_w.at[1], merged.at[source], coefs, rows_total, rows)
-
-    forward(0)
-
+        first_sq, _ = replica_grad(0, source * 2 + y)
+        for half in range(2):
+            copy_of(source * 2 + 1 - y, half, 2, other).wait_recv()
+        second_sq, cross = replica_grad(1, source * 2 + 1 - y)
+        coefs = coefs_of(first_sq, second_sq, cross)
+        lower, upper, target = pair_w.at[0], pair_w.at[1], source
+        rest = k + 1
+        while True:
+            against = merged.at[stack[-1]] if rest % 2 == 0 else None
+            coefs = pair_merge(lower, upper, merged.at[target], coefs, against, rows_total, rows)
+            if against is None:
+                stack.append(target)
+                return None
+            lower, upper = merged.at[target], against
+            target = stack.pop()
+            rest //= 2
+            if k == chain - 1 and not stack:
+                return lower, upper, coefs
+
+    forward(0, (0,))
+    z_f = pre_ref[...].astype(F32)
+    sig = jax.nn.sigmoid(z_f)
+    factors[rep, 1] = (up_ref[...].astype(F32) * sig * (1.0 + z_f * (1.0 - sig))).astype(BF16)
     spread(rep)
-    loads[0].wait()
+    forward(0, (1,))
+    load.wait()
     total = jnp.zeros((pixels, channels), F32)
     for i in range(3):
         for j in range(3):
@@ -302,36 +313,12 @@
             def _():
                 passing.start()
         process(k - 1)
-    if chain == 1:
-        @pl.when(pipe > 0)
-        def _():
-            passing.start()
-    process(chain - 1)
-
-    stride = 1
-    while stride * 2 < chain:
-        for low in range(0, chain, stride * 2):
-            pair = merged.at[low], merged.at[low + stride]
-            coefs = pair_dots(*pair, rows_total, rows)
-            pair_merge(*pair, merged.at[low], coefs, rows_total, rows)
-        stride *= 2
-    for load in loads[1:]:
-        load.wait()
+    lower, upper, coefs = process(chain - 1)
+
     own_rows = rows_total // replicas
     own = pl.ds(pl.multiple_of(rep * own_rows, own_rows), own_rows)
-    if stride < chain:
-        coefs = pair_dots(merged.at[0], merged.at[stride], rows_total, rows)
-        final = coefs[0] * merged[0, own, :].astype(F32) + coefs[1] * merged[stride, own, :].astype(F32)
-        final = final.astype(BF16).astype(F32)
-    else:
-        final = merged[0, own, :].astype(F32)
-    lanes = momentum_v.shape[-1]
-    groups = channels // lanes
-    for g in range(groups):
-        at = pl.ds(g, own_rows, stride=groups)
-        momentum = 0.9 * momentum_v[at, :] + 0.0625 * final[:, g * lanes : (g + 1) * lanes]
-        new_mom_ref[at, :] = momentum
-        new_w_ref[at, :] = master_v[at, :] - 0.02 * momentum
+    final = coefs[0] * lower[own, :].astype(F32) + coefs[1] * upper[own, :].astype(F32)
+    combined_ref[...] = final.astype(BF16)
 
     for k in range(chain):
         source = sources[k]
@@ -352,6 +339,19 @@
         passing.wait_recv()
 
 
+def update(combined, master, momentum, passed_in, new_momentum, new_weights, passed_out):
+    own_rows, channels = combined.shape
+    lanes = momentum.shape[-1]
+    groups = channels // lanes
+    passed_out[...] = passed_in[...]
+    for g in range(groups):
+        at = pl.ds(g, own_rows, stride=groups)
+        part = combined[:, g * lanes : (g + 1) * lanes].astype(F32)
+        moved = 0.9 * momentum[at, :] + 0.0625 * part
+        new_momentum[at, :] = moved
+        new_weights[at, :] = master[at, :] - 0.02 * moved
+
+
 def factor_body(sections, replicas, activations, preactivation, upstream, weights, master, momentum):
     tile = activations.shape[3:]
     cols, channels = tile[1], tile[2]
@@ -360,15 +360,14 @@
     lanes = 128
     flat = (momentum.shape[2] // lanes, lanes)
     small, big = pl.BlockSpec(memory_space=pltpu.VMEM), pl.BlockSpec(memory_space=pl.ANY)
-    passed, new_momentum, new_weights = pl.pallas_call(
+    passed, combined = pl.pallas_call(
         functools.partial(kernel, sections, replicas, cols),
         out_shape=(
             jax.ShapeDtypeStruct((pixels, channels), BF16),
-            jax.ShapeDtypeStruct(flat, F32),
-            jax.ShapeDtypeStruct(flat, F32),
+            jax.ShapeDtypeStruct((taps_rows // replicas, channels), BF16),
         ),
-        in_specs=[small, small, small, big, big, big],
-        out_specs=(small, small, small),
+        in_specs=[small, small, small, big],
+        out_specs=(small, small),
         scratch_shapes=[
             pltpu.VMEM((replicas, 2, pixels, channels), BF16),
             pltpu.VMEM((3, pixels + 2 * cols, channels), BF16),
@@ -377,12 +376,10 @@
             pltpu.VMEM((pixels, channels), BF16),
             pltpu.VMEM((2, taps_rows, channels), BF16),
             pltpu.VMEM((replicas // 2, taps_rows, channels), BF16),
-            pltpu.VMEM(flat, F32),
-            pltpu.VMEM(flat, F32),
             pltpu.SemaphoreType.DMA((3, replicas, 2)),
             pltpu.SemaphoreType.DMA((replicas, 2)),
             pltpu.SemaphoreType.DMA((2,)),
-            pltpu.SemaphoreType.DMA((3,)),
+            pltpu.SemaphoreType.DMA,
         ],
         compiler_params=pltpu.CompilerParams(
             collective_id=0, has_side_effects=True, vmem_limit_bytes=56 * 1024 * 1024
@@ -392,9 +389,17 @@
         preactivation.reshape(pixels, channels),
         upstream.reshape(pixels, channels),
         weights[0],
-        master.reshape(flat),
-        momentum.reshape(flat),
-    )
+    )
+    new_momentum, new_weights, passed = pl.pallas_call(
+        update,
+        out_shape=(
+            jax.ShapeDtypeStruct(flat, F32),
+            jax.ShapeDtypeStruct(flat, F32),
+            jax.ShapeDtypeStruct((pixels, channels), BF16),
+        ),
+        in_specs=[small] * 4,
+        out_specs=(small,) * 3,
+    )(combined, master.reshape(flat), momentum.reshape(flat), passed)
     return (
         passed.reshape(activations.shape),
         new_momentum.reshape(momentum.shape),
@@ -406,7 +411,8 @@
     activations, weights, momentum = arrays[0], arrays[3], arrays[5]
     factor = 2 * activations.size
     fits = (
-        replicas >= 2
+        replicas >= 4
+        and replicas & (replicas - 1) == 0
         and activations.shape[2] == 1
         and (replicas - 1) * factor <= 2 * weights.size
         and activations.shape[4] % 16 == 0

time: 62.5 us -> 57.5 us (0.920)
  local copies, waits for them, and re-layouts: 5.29 us -> 0 us
    unnamed x3 -> x0, local copies, waits for them, and re-layouts: 5.29 us -> none
    pallas_call x0 -> x1, Pallas kernels: none -> 2.76 us  [factor_body(): pl.pallas_call(update, out_shape=(jax.ShapeDtypeStruct(flat, F32), jax.Sh...]
    pallas_call x1, Pallas kernels: 56.4 us -> 53.9 us  [factor_body(): pl.pallas_call(functools.partial(kernel, sections, replicas, cols), out_s...]
where the time goes in v2:
time: 57.5 us; the launch traced here: 57.3 us
  Pallas kernels  56.7 us (99%)
  between operations  0.64 us (1%)
    pallas_call x1, Pallas kernels, factor_body(): pl.pallas_call(functools.partial(kernel, sections, replicas, cols), out_s...  53.9 us
    pallas_call x1, Pallas kernels, factor_body(): pl.pallas_call(update, out_shape=(jax.ShapeDtypeStruct(flat, F32), jax.Sh...  2.76 us

profile of v2, /device:TPU:0, one launch (start us, length us, event | category | flops | bytes accessed | tf_op | source)
XLA Modules:
  0.0 57.3 jit_solution(17025245634593266761)
XLA Ops:
  0.6 53.9 %shard_map.85 = (bf16[256,384]{1,0:T(8,128)(2,1)}, bf16[432,384]{1,0:T(8,128)(2,1)}) custom-call(bf16[256,384]{1,0:T(8,128)(2,1)} %bitcast.12, bf16[256,384]{1,0:T(8,128)(2,1)} %bitcast.13, bf16[256,384]{1,0:T(8,128)(2,1)} %bitcast.14, bf16[3456,384]{1,0:T(8,128)(2,1)} %bitcast.9), custom_call_target="tpu_custom_call" | custom-call | tf_op jit(solution)/shard_map/pallas_call | solution.py:363
  54.5 2.8 %shard_map.86 = (f32[1296,128]{1,0:T(8,128)}, f32[1296,128]{1,0:T(8,128)}, bf16[256,384]{1,0:T(8,128)(2,1)}) custom-call(bf16[432,384]{1,0:T(8,128)(2,1)} %get-tuple-element.8.combined, f32[1296,128]{1,0:T(8,128)} %bitcast.10, f32[1296,128]{1,0:T(8,128)} %bitcast.11, bf16[256,384]{1,0:T(8,128)(2,1)} %get-tuple-element.9.passed_in), custom_call_target="tpu_custom_call" | custom-call | tf_op jit(solution)/shard_map/pallas_call | solution.py:393

commit v3 on v2

--- a/solution.py
+++ b/solution.py
@@ -141,7 +141,8 @@
 
     zero = jnp.zeros((8, channels), F32)
     init = () if against is None else (zero, zero, zero)
-    sums = lax.fori_loop(0, rows_total // rows, step, init)
+    count = rows_total // rows
+    sums = lax.fori_loop(0, count, step, init, unroll=next(n for n in (3, 2, 1) if count % n == 0))
     return None if against is None else coefs_of(*sums)
 
 
@@ -254,9 +255,11 @@
 
     stack = []
 
-    def process(k):
+    def first(k):
+        return replica_grad(0, sources[k] * 2 + y)[0]
+
+    def second(k, first_sq):
         source = sources[k]
-        first_sq, _ = replica_grad(0, source * 2 + y)
         for half in range(2):
             copy_of(source * 2 + 1 - y, half, 2, other).wait_recv()
         second_sq, cross = replica_grad(1, source * 2 + 1 - y)
@@ -306,14 +309,27 @@
         device_id_type=MESH,
     )
 
+    first_sq = first(0)
+    forward(1)
+
+    @pl.when(pipe > 0)
+    def _():
+        passing.start()
+
+    for k in range(2, chain):
+        @pl.when(jnp.abs(sources[k] - z) == 1)
+        def _():
+            forward(k)
+
+    second(0, first_sq)
     for k in range(1, chain):
-        forward(k)
-        if k == 1:
-            @pl.when(pipe > 0)
+        first_sq = first(k)
+        if k + 1 < chain:
+            @pl.when(jnp.abs(sources[k + 1] - z) != 1)
             def _():
-                passing.start()
-        process(k - 1)
-    lower, upper, coefs = process(chain - 1)
+                forward(k + 1)
+        result = second(k, first_sq)
+    lower, upper, coefs = result
 
     own_rows = rows_total // replicas
     own = pl.ds(pl.multiple_of(rep * own_rows, own_rows), own_rows)

time: 57.5 us -> 57.1 us (level)
  no operation moved by 1% of the time
where the time goes in v3:
time: 57.1 us; the launch traced here: 56.9 us
  Pallas kernels  56.3 us (99%)
  between operations  0.64 us (1%)
    pallas_call x1, Pallas kernels, factor_body(): pl.pallas_call(functools.partial(kernel, sections, replicas, cols), out_s...  53.5 us
    pallas_call x1, Pallas kernels, factor_body(): pl.pallas_call(update, out_shape=(jax.ShapeDtypeStruct(flat, F32), jax.Sh...  2.76 us

profile of v3, /device:TPU:0, one launch (start us, length us, event | category | flops | bytes accessed | tf_op | source)
XLA Modules:
  0.0 56.9 jit_solution(11548855237094156314)
XLA Ops:
  0.6 53.5 %shard_map.85 = (bf16[256,384]{1,0:T(8,128)(2,1)}, bf16[432,384]{1,0:T(8,128)(2,1)}) custom-call(bf16[256,384]{1,0:T(8,128)(2,1)} %bitcast.12, bf16[256,384]{1,0:T(8,128)(2,1)} %bitcast.13, bf16[256,384]{1,0:T(8,128)(2,1)} %bitcast.14, bf16[3456,384]{1,0:T(8,128)(2,1)} %bitcast.9), custom_call_target="tpu_custom_call" | custom-call | tf_op jit(solution)/shard_map/pallas_call | solution.py:379
  54.1 2.8 %shard_map.86 = (f32[1296,128]{1,0:T(8,128)}, f32[1296,128]{1,0:T(8,128)}, bf16[256,384]{1,0:T(8,128)(2,1)}) custom-call(bf16[432,384]{1,0:T(8,128)(2,1)} %get-tuple-element.8.combined, f32[1296,128]{1,0:T(8,128)} %bitcast.10, f32[1296,128]{1,0:T(8,128)} %bitcast.11, bf16[256,384]{1,0:T(8,128)(2,1)} %get-tuple-element.9.passed_in), custom_call_target="tpu_custom_call" | custom-call | tf_op jit(solution)/shard_map/pallas_call | solution.py:409

commit v4 on v3

--- a/solution.py
+++ b/solution.py
@@ -110,7 +110,7 @@
 
 
 def chunk_rows(channels):
-    return next(rows for rows in (64, 48, 32, 16) if channels % rows == 0)
+    return next(rows for rows in (32, 16) if channels % rows == 0)
 
 
 def fold(product):

time: 57.1 us -> 57.7 us (1.011)
  Pallas kernels: 56.3 us -> 56.9 us
    pallas_call x1, Pallas kernels: 53.5 us -> 54.1 us  [factor_body(): pl.pallas_call(functools.partial(kernel, sections, replicas, cols), out_s...]
where the time goes in v4:
time: 57.7 us; the launch traced here: 57.5 us
  Pallas kernels  56.9 us (99%)
  between operations  0.64 us (1%)
    pallas_call x1, Pallas kernels, factor_body(): pl.pallas_call(functools.partial(kernel, sections, replicas, cols), out_s...  54.1 us
    pallas_call x1, Pallas kernels, factor_body(): pl.pallas_call(update, out_shape=(jax.ShapeDtypeStruct(flat, F32), jax.Sh...  2.76 us

profile of v4, /device:TPU:0, one launch (start us, length us, event | category | flops | bytes accessed | tf_op | source)
XLA Modules:
  0.0 57.5 jit_solution(6666153026865553521)
XLA Ops:
  0.6 54.1 %shard_map.85 = (bf16[256,384]{1,0:T(8,128)(2,1)}, bf16[432,384]{1,0:T(8,128)(2,1)}) custom-call(bf16[256,384]{1,0:T(8,128)(2,1)} %bitcast.12, bf16[256,384]{1,0:T(8,128)(2,1)} %bitcast.13, bf16[256,384]{1,0:T(8,128)(2,1)} %bitcast.14, bf16[3456,384]{1,0:T(8,128)(2,1)} %bitcast.9), custom_call_target="tpu_custom_call" | custom-call | tf_op jit(solution)/shard_map/pallas_call | solution.py:379
  54.8 2.8 %shard_map.86 = (f32[1296,128]{1,0:T(8,128)}, f32[1296,128]{1,0:T(8,128)}, bf16[256,384]{1,0:T(8,128)(2,1)}) custom-call(bf16[432,384]{1,0:T(8,128)(2,1)} %get-tuple-element.8.combined, f32[1296,128]{1,0:T(8,128)} %bitcast.10, f32[1296,128]{1,0:T(8,128)} %bitcast.11, bf16[256,384]{1,0:T(8,128)(2,1)} %get-tuple-element.9.passed_in), custom_call_target="tpu_custom_call" | custom-call | tf_op jit(solution)/shard_map/pallas_call | solution.py:409
